TPU v7x, 256 devices: a whole 4x4x8 slice. The times are simulated.
256 devices in a mesh: row: 32 (over x, z_hi, core), col: 8 (over y, z_lo).
Axes of the slice: x: 4, y: 4, z: 8 (z_hi: 4, z_lo: 2; z = z_hi * 2 + z_lo), core: 2. Of those that a mesh axis runs over, the one named last changes fastest.
Arguments:
- sigma_anc: float32 [128, 128, 128, 128], P('row', 'col'), as said below
- panel: float32 [2, 128, 128, 512], P(None, 'row'), may hold values from -0.12 to 0.12
- pattern: int32 [2, 64], replicated, may hold values from 0 to 127, as said below
- linv: float32 [2, 512, 512], replicated, as said below
Outputs:
- sigma_sj: float32 [2, 128, 128, 512], P(None, 'row')
- sigma_jj: float32 [2, 512, 512], replicated
Inputs may be any that keep to these rules, and one draw needn't show every extreme that they name: `pattern`: each row lists 64 distinct ancestor block indices in increasing order; 0 and 127 are always among them. `sigma_anc`: symmetric as a matrix of order 128 * 128 in ancestor order. `linv`: lower triangular, diagonal entries between 1 and 2.
All inputs are finite; a program needn't handle non-finite values.
Results may differ from a plain program's by a relative error of at most 0.0001.
Values sent between devices are 32-bit elements; how exact they have to be, the bound alone decides.
A program may use at most 128 MiB of HBM per device.

v0:
```python
import jax
import jax.numpy as jnp
from jax import lax
from jax.sharding import PartitionSpec as P


def local(sigma_anc, panel, pattern, linv):
    highest = lax.Precision.HIGHEST
    rows_here = sigma_anc.shape[0]
    cols_here = sigma_anc.shape[1]
    row_count = lax.axis_size("row")
    col_count = lax.axis_size("col")
    row_index = lax.axis_index("row")
    column_index = lax.axis_index("col")
    row_ids = jnp.arange(rows_here, dtype=jnp.int32) * row_count + row_index
    col_ids = jnp.arange(cols_here, dtype=jnp.int32) * col_count + column_index
    in_pattern = jnp.any(pattern[:, :, None] == row_ids[None, None, :], axis=1).astype(jnp.float32)
    updated = jnp.einsum(
        "sqiw,swv->sqiv", panel, linv, precision=highest, preferred_element_type=jnp.float32
    )
    updated = updated * in_pattern[:, :, None, None]
    selector = (col_ids[:, None] == row_ids[None, :]).astype(jnp.float32)
    local_cols = jnp.einsum(
        "kq,sqiw->skiw", selector, updated, precision=highest, preferred_element_type=jnp.float32
    )
    gathered_cols = lax.psum(local_cols, "row")
    partial_value = jnp.einsum(
        "qkij,skjw->sqiw",
        sigma_anc,
        gathered_cols,
        precision=highest,
        preferred_element_type=jnp.float32,
    )
    product = lax.psum(partial_value, "col")
    product = product * in_pattern[:, :, None, None]
    sigma_sj = -product
    base_term = jnp.einsum(
        "siw,siv->swv", linv, linv, precision=highest, preferred_element_type=jnp.float32
    )
    local_term = jnp.einsum(
        "sqiw,sqiv->swv", updated, product, precision=highest, preferred_element_type=jnp.float32
    )
    total_term = lax.psum(local_term, "row")
    sigma_jj = base_term + total_term
    return (sigma_sj, sigma_jj)


def solution(mesh):
    return jax.shard_map(
        local,
        mesh=mesh,
        in_specs=(P("row", "col", None, None), P(None, "row", None, None), P(), P()),
        out_specs=(P(None, "row", None, None), P()),
        check_vma=False,
    )
```

profile of v0, /device:TPU:1, one launch (start us, length us, event | category | flops | bytes accessed | tf_op | source)
XLA Modules:
  0.0 793.9 jit_solution(9738361498573340036)
XLA Ops:
  7.2 0.0 copy-start
  7.2 0.0 all-reduce.4.cloned.1.call-start
  7.3 1.0 compare_reduce_fusion
  8.3 0.5 copy-done
  8.8 5.1 fusion.12
  13.9 0.0 copy-start.1
  13.9 1.3 copy-done.1
  15.2 6.0 fusion.5
  21.2 10.0 %copy.15 = f32[2,128,512,16]{1,2,3,0:T(8,128)} copy(f32[2,128,512,16]{2,3,1,0:T(8,128)} %fusion.5) | data formatting | bytes 16777216 | tf_op jit(solution)/shard_map/kq,sqiw->skiw/dot_general | solution.py:23
  31.2 0.0 all-reduce.4.cloned.1.call-update
  31.2 0.2 all-reduce.6.cloned.1.call-start
  31.5 328.1 %all-reduce.4.cloned.1.call-done = f32[2,16,128,512]{2,3,1,0:T(8,128)} async-done(((f32[2,16,128,512]{2,3,1,0:T(8,128)}), f32[2,16,128,512]{2,3,1,0:T(8,128)}) %all-reduce.4.cloned.1.call-update) | async-done | bytes 8388624 | tf_op jit(solution)/shard_map/psum | solution.py:26
  359.6 17.7 %fusion.15 = f32[2,4,128,512]{3,2,1,0:T(8,128)} fusion(f32[4,16,128,128]{3,2,1,0:T(8,128)} %param.4, f32[2,16,128,512]{2,3,1,0:T(8,128)} %all-reduce.4.cloned.1.call-done), kind=kOutput, calls=%fused_computation.12 | convolution fusion | flops 12884901888 | bytes 14680064 | tf_op jit(solution)/shard_map/qkij,skjw->sqiw/dot_general | solution.py:27
  377.3 0.0 all-reduce.6.cloned.1.call-update
  377.4 0.3 all-reduce.8.cloned.1.call-start
  377.6 107.8 %all-reduce.6.cloned.1.call-done = f32[2,4,128,512]{3,2,1,0:T(8,128)} async-done(((f32[2,4,128,512]{3,2,1,0:T(8,128)}), f32[2,4,128,512]{3,2,1,0:T(8,128)}) %all-reduce.6.cloned.1.call-update) | async-done | bytes 2097168 | tf_op jit(solution)/shard_map/psum | solution.py:34
  485.4 7.4 fusion.9
  492.8 0.0 all-reduce.8.cloned.1.call-update
  492.8 3.4 multiply_negate_fusion
  496.2 285.3 %all-reduce.8.cloned.1.call-done = f32[2,512,512]{2,1,0:T(8,128)} async-done(((f32[2,512,512]{2,1,0:T(8,128)}), f32[2,512,512]{2,1,0:T(8,128)}) %all-reduce.8.cloned.1.call-update) | async-done | bytes 2097168 | tf_op jit(solution)/shard_map/psum | solution.py:43
  781.4 5.9 convolution_add_fusion
  (3 shorter events, 0.0 us)
Async XLA Ops:
  7.2 1.6 copy-start
  7.2 352.4 %all-reduce.4.cloned.1.call-start = ((), (), s32[]{:S(2)}) async-start(), calls=%async_computation | async-start | bytes 16777216 | tf_op jit(solution)/shard_map/psum | solution.py:26
  13.9 1.3 copy-start.1
  31.2 454.2 %all-reduce.6.cloned.1.call-start = ((), (), s32[]{:S(2)}) async-start(), calls=%async_computation.1 | async-start | bytes 4194304 | tf_op jit(solution)/shard_map/psum | solution.py:34
  377.4 404.1 %all-reduce.8.cloned.1.call-start = ((), (), s32[]{:S(2)}) async-start(), calls=%async_computation.2 | async-start | bytes 4194304 | tf_op jit(solution)/shard_map/psum | solution.py:43
Sparse Core Ops, SparseCore 0:
  31.4 328.1 all-reduce.3
  377.5 107.8 all-reduce.5
  492.9 288.4 all-reduce.7
where the time goes:
time: 794 us
  waiting for transfers between devices  721 us (91%)
  matrix products  42.1 us (5%)
  between operations  13.8 us (2%)
  local copies, waits for them, and re-layouts  11.9 us (1%)
    psum x1, waiting for transfers between devices, local(): gathered_cols = lax.psum(local_cols, 'row')  328 us
    psum x1, waiting for transfers between devices, local(): total_term = lax.psum(local_term, 'row')  285 us
    psum x1, waiting for transfers between devices, local(): product = lax.psum(partial_value, 'col')  108 us
    dot_general x1, matrix products, local(): jnp.einsum('qkij,skjw->sqiw', sigma_anc, gathered_cols, precision=highest...  17.7 us
  transfers between devices with their start and end apart: 3, of which 3 were waited for; matrix products, arithmetic and copies ran while one was open for 0% of the time, Pallas kernels for 0%

commit v1 on v0

--- a/solution.py
+++ b/solution.py
@@ -40,7 +40,7 @@
     local_term = jnp.einsum(
         "sqiw,sqiv->swv", updated, product, precision=highest, preferred_element_type=jnp.float32
     )
-    total_term = lax.psum(local_term, "row")
+    total_term = jnp.sum(lax.all_gather(local_term, "row"), axis=0)
     sigma_jj = base_term + total_term
     return (sigma_sj, sigma_jj)
 

time: 794 us -> 894 us (1.13)
  waiting for transfers between devices: 721 us -> 803 us
  other arithmetic: 4.37 us -> 26.6 us
    all_gather x0 -> x1, waiting for transfers between devices: none -> 374 us  [local(): total_term = jnp.sum(lax.all_gather(local_term, 'row'), axis=0)]
    psum x1 -> x0, waiting for transfers between devices: 285 us -> none  [local(): total_term = lax.psum(local_term, 'row')]
    reduce_sum x0 -> x1, other arithmetic: none -> 22.2 us  [local(): total_term = jnp.sum(lax.all_gather(local_term, 'row'), axis=0)]
    dot_general x1 -> x0, local copies, waits for them, and re-layouts: 10 us -> none  [local(): jnp.einsum('kq,sqiw->skiw', selector, updated, precision=highest, preferr...]
  transfers between devices with their start and end apart: 3 -> 3, of which waited for: 3 -> 3; matrix products, arithmetic and copies ran while one was open for 0% -> 1% of each run, Pallas kernels for 0% -> 0%
where the time goes in v1:
time: 894 us
  waiting for transfers between devices  803 us (90%)
  matrix products  42.5 us (5%)
  other arithmetic  26.6 us (3%)
  between operations  13.8 us (2%)
    all_gather x1, waiting for transfers between devices, local(): total_term = jnp.sum(lax.all_gather(local_term, 'row'), axis=0)  374 us
    psum x1, waiting for transfers between devices, local(): gathered_cols = lax.psum(local_cols, 'row')  321 us
    psum x1, waiting for transfers between devices, local(): product = lax.psum(partial_value, 'col')  108 us
    reduce_sum x1, other arithmetic, local(): total_term = jnp.sum(lax.all_gather(local_term, 'row'), axis=0)  22.2 us
    dot_general x1, matrix products, local(): jnp.einsum('qkij,skjw->sqiw', sigma_anc, gathered_cols, precision=highest...  18 us
  transfers between devices with their start and end apart: 3, of which 3 were waited for; matrix products, arithmetic and copies ran while one was open for 1% of the time, Pallas kernels for 0%

profile of v1, /device:TPU:1, one launch (start us, length us, event | category | flops | bytes accessed | tf_op | source)
XLA Modules:
  0.0 893.8 jit_solution(10784491128204240918)
XLA Ops:
  7.2 0.0 copy-start
  7.2 0.0 all-reduce.3.cloned.1.call-start
  7.3 1.0 compare_reduce_fusion
  8.3 0.5 copy-done
  8.8 5.1 fusion.13
  13.9 0.0 copy-start.1
  13.9 1.3 copy-done.1
  15.2 6.1 convolution_bitcast_fusion
  21.3 0.0 all-reduce.3.cloned.1.call-update
  21.3 0.2 all-reduce.5.cloned.1.call-start
  21.6 5.4 copy.20
  27.0 321.5 %all-reduce.3.cloned.1.call-done = f32[2,16,128,512]{3,1,2,0:T(8,128)} async-done(((f32[2,16,128,512]{3,1,2,0:T(8,128)}), f32[2,16,128,512]{3,1,2,0:T(8,128)}) %all-reduce.3.cloned.1.call-update) | async-done | bytes 8388624 | tf_op jit(solution)/shard_map/psum | solution.py:26
  348.5 18.0 %fusion.7 = f32[2,4,128,512]{3,2,1,0:T(8,128)} fusion(f32[4,16,128,128,1]{2,1,3,0,4:T(8,128)} %copy.20, f32[2,16,128,512]{3,1,2,0:T(8,128)} %all-reduce.3.cloned.1.call-done), kind=kOutput, calls=%fused_computation.9 | convolution fusion | flops 12884901888 | bytes 14680064 | tf_op jit(solution)/shard_map/qkij,skjw->sqiw/dot_general | solution.py:27
  366.5 0.0 all-reduce.5.cloned.1.call-update
  366.5 0.3 all-gather.3.cloned.1.call-start
  366.8 107.8 %all-reduce.5.cloned.1.call-done = f32[2,4,128,512]{3,2,1,0:T(8,128)} async-done(((f32[2,4,128,512]{3,2,1,0:T(8,128)}), f32[2,4,128,512]{3,2,1,0:T(8,128)}) %all-reduce.5.cloned.1.call-update) | async-done | bytes 2097168 | tf_op jit(solution)/shard_map/psum | solution.py:34
  474.6 7.4 fusion.10
  481.9 0.0 all-gather.3.cloned.1.call-update
  482.0 3.4 multiply_negate_fusion
  485.3 373.8 %all-gather.3.cloned.1.call-done = f32[64,512,512]{2,1,0:T(8,128)} async-done(((f32[2,512,512]{2,1,0:T(8,128)}), f32[64,512,512]{2,1,0:T(8,128)}) %all-gather.3.cloned.1.call-update) | async-done | bytes 67108880 | tf_op jit(solution)/shard_map/all_gather | solution.py:43
  859.1 22.2 %reduce_sum.9 = f32[2,512,512]{2,1,0:T(8,128)} reduce(f32[32,2,512,512]{3,2,1,0:T(8,128)} %bitcast.11, f32[]{:T(128)} %constant.16.clone.1), dimensions={0}, to_apply=%region_3.0 | reduce | flops 16252928 | bytes 69206016 | tf_op jit(solution)/shard_map/reduce_sum | solution.py:43
  881.4 5.9 convolution_add_fusion
  (3 shorter events, 0.0 us)
Async XLA Ops:
  7.2 1.6 copy-start
  7.2 341.3 %all-reduce.3.cloned.1.call-start = ((), (), s32[]{:S(2)}) async-start(), calls=%async_computation | async-start | bytes 16777216 | tf_op jit(solution)/shard_map/psum | solution.py:26
  13.9 1.3 copy-start.1
  21.3 453.2 %all-reduce.5.cloned.1.call-start = ((), (), s32[]{:S(2)}) async-start(), calls=%async_computation.1 | async-start | bytes 4194304 | tf_op jit(solution)/shard_map/psum | solution.py:34
  366.5 492.6 %all-gather.3.cloned.1.call-start = ((), (), s32[]{:S(2)}) async-start(), calls=%async_computation.2 | async-start | bytes 69206016 | tf_op jit(solution)/shard_map/all_gather | solution.py:43
Sparse Core Ops, SparseCore 0:
  21.5 326.9 all-reduce.2
  366.6 107.8 all-reduce.4
  482.1 377.0 all-gather.2
